TPU v7x, 32 devices: a whole 2x2x4 slice. The times are simulated.
32 devices in a mesh: depth: 4 (over z), wide: 8 (over y, x, core).
Axes of the slice: x: 2, y: 2, z: 4, core: 2. Of those that a mesh axis runs over, the one named last changes fastest.
Arguments:
- density: float32 [4, 4096, 4096], P('depth', 'wide'), may hold values from -4 to 4
- layer_top: float32 [4], P('depth'), may hold values from 0.75 to 1.5
- layer_thick: float32 [4], P('depth'), may hold values from 1.5 to 3
- sample_row: int32 [32, 256], P(('depth', 'wide')), may hold values from 0 to 127
- sample_col: int32 [32, 256], P(('depth', 'wide')), may hold values from 0 to 4095
- sample_frac: int32 [32, 2, 256], P(('depth', 'wide')), may hold values from 0 to 15
- sample_owner: int32 [32, 256, 1], P(('depth', 'wide')), may hold values from 0 to 7; in each aligned block of 256 rows (0 to 255, 256 to 511, ..., all dimensions but the last counted through in order) at most 64 rows name the same one
Outputs:
- gradient_grid: float32 [6, 4096, 4096], P(None, ('depth', 'wide'))
- line_samples: float32 [6, 32, 512], P(None, ('depth', 'wide'))
Inputs may be any that keep to these rules, and one draw needn't show every extreme that they name: `sample_owner`: among the 256 samples of one tile no owner is named more than 64 times, a bound that some block reaches.
All inputs are finite; a program needn't handle non-finite values.
Results may differ from a plain program's by a relative error of at most 0.0001.
Values sent between devices are 32-bit elements; how exact they have to be, the bound alone decides.
No kernel may reach another device: no remote copies, remote signals or barrier semaphores. Data moves between devices by JAX's collectives and lax.ppermute only.
A program may use at most 320 MiB of HBM per device.

v0:
```python
import math
import jax
import jax.numpy as jnp
from jax import lax
from jax.sharding import PartitionSpec as P

RADIX = 128
QLEV = 16
HIGH = lax.Precision.HIGHEST


def padded_2(block, sides, width):
    for axis, dim in sides:
        count = lax.axis_size(axis)
        forward = [(i, i + 1) for i in range(count - 1)]
        forward.append((count - 1, 0))
        backward = [(target, source) for source, target in forward]
        low = lax.ppermute(
            lax.slice_in_dim(block, block.shape[dim] - width, None, axis=dim), axis, forward
        )
        high = lax.ppermute(lax.slice_in_dim(block, 0, width, axis=dim), axis, backward)
        block = jnp.concatenate([low, block, high], axis=dim)
    return block


def product(formula, operand_a, operand_b):
    return jnp.einsum(formula, operand_a, operand_b, precision=HIGH)


def complex_product(formula, complex_pair, table_pair):
    real_part = product(formula, complex_pair[0], table_pair[0]) - product(
        formula, complex_pair[1], table_pair[1]
    )
    imag_part = product(formula, complex_pair[0], table_pair[1]) + product(
        formula, complex_pair[1], table_pair[0]
    )
    return (real_part, imag_part)


def phase_table(row_count, col_count, period, orient):
    left_ids = jnp.arange(row_count, dtype=jnp.int32)[:, None]
    right_ids = jnp.arange(col_count, dtype=jnp.int32)[None, :]
    angles = (left_ids * right_ids % period).astype(jnp.float32) * (2.0 * math.pi / period)
    return (jnp.cos(angles), orient * jnp.sin(angles))


def times_table(complex_pair, table_pair):
    return (
        complex_pair[0] * table_pair[0] - complex_pair[1] * table_pair[1],
        complex_pair[0] * table_pair[1] + complex_pair[1] * table_pair[0],
    )


def column_forward(complex_pair):
    grid_len = complex_pair[0].shape[0]
    outer_len = grid_len // RADIX
    item_count = complex_pair[0].shape[2]
    columns = (
        complex_pair[0].reshape(outer_len, RADIX, item_count),
        complex_pair[1].reshape(outer_len, RADIX, item_count),
    )
    partial_value = complex_product(
        "bcd,ab->acd", columns, phase_table(outer_len, outer_len, outer_len, -1.0)
    )
    twiddles = phase_table(outer_len, RADIX, grid_len, -1.0)
    partial_value = times_table(partial_value, (twiddles[0][:, :, None], twiddles[1][:, :, None]))
    return complex_product("abd,bc->acd", partial_value, phase_table(RADIX, RADIX, RADIX, -1.0))


def row_inverse(complex_pair):
    dims_in = complex_pair[0].shape
    grid_len = dims_in[-1]
    outer_len = grid_len // RADIX
    flat_dims = (-1, outer_len, RADIX)
    row_values = (complex_pair[0].reshape(flat_dims), complex_pair[1].reshape(flat_dims))
    partial_value = complex_product(
        "zab,cb->zac", row_values, phase_table(RADIX, RADIX, RADIX, 1.0)
    )
    partial_value = times_table(partial_value, phase_table(outer_len, RADIX, grid_len, 1.0))
    partial_value = complex_product(
        "zbc,ab->zac", partial_value, phase_table(outer_len, outer_len, outer_len, 1.0)
    )
    return (partial_value[0].reshape(dims_in), partial_value[1].reshape(dims_in))


def column_inverse_start(complex_pair):
    outer_len = complex_pair[0].shape[1]
    partial_value = complex_product(
        "jabd,cb->jacd", complex_pair, phase_table(RADIX, RADIX, RADIX, 1.0)
    )
    twiddles = phase_table(outer_len, RADIX, outer_len * RADIX, 1.0)
    return times_table(partial_value, (twiddles[0][:, :, None], twiddles[1][:, :, None]))


def wavenumber(wave_index, grid_len):
    signed_ids = jnp.where(wave_index < grid_len // 2, wave_index, wave_index - grid_len).astype(
        jnp.float32
    )
    full_wave = signed_ids * (2.0 * math.pi / grid_len)
    odd_wave = jnp.where(wave_index == grid_len // 2, 0.0, full_wave)
    return (full_wave, odd_wave)


def channel_spectra(continued, full_x, full_y, odd_x, odd_y, safe_square, safe_root):
    real_part, imag_part = continued
    coef_xx = -full_x * full_x / safe_square
    coef_yy = -full_y * full_y / safe_square
    coef_xy = -odd_x * odd_y / safe_square
    slope_x = odd_x / safe_root
    slope_y = odd_y / safe_root
    first_pair = (
        real_part * coef_xx - imag_part * coef_yy,
        real_part * coef_yy + imag_part * coef_xx,
    )
    second_pair = (real_part * coef_xy - imag_part, real_part + imag_part * coef_xy)
    third_pair = (
        -real_part * slope_y - imag_part * slope_x,
        real_part * slope_x - imag_part * slope_y,
    )
    return (
        jnp.stack([first_pair[0], second_pair[0], third_pair[0]]),
        jnp.stack([first_pair[1], second_pair[1], third_pair[1]]),
    )


def ordered_channels(real_fields, imag_fields):
    return jnp.concatenate(
        [real_fields, imag_fields[0:1], imag_fields[2:3], imag_fields[1:2]], axis=0
    )


def cubic_kernel(distance):
    near_part = (1.5 * distance - 2.5) * distance * distance + 1.0
    far_part = ((-0.5 * distance + 2.5) * distance - 4.0) * distance + 2.0
    return jnp.where(distance <= 1.0, near_part, jnp.where(distance < 2.0, far_part, 0.0))


def weight_rows(levels):
    level_ids = jnp.arange(levels, dtype=jnp.int32)
    offsets = (level_ids.astype(jnp.float32) + 0.5) / levels - 0.5
    bases = jnp.where(level_ids < levels // 2, -1.0, 0.0).astype(jnp.float32)
    fraction = offsets - bases
    tap_pos = jnp.arange(4, dtype=jnp.int32).astype(jnp.float32) - 1.0
    return cubic_kernel(jnp.abs(fraction[:, None] - tap_pos[None, :]))


def per_device(density, layer_top, layer_thick, sample_row, sample_col, sample_frac, sample_owner):
    wide_count = lax.axis_size("wide")
    depth_count = lax.axis_size("depth")
    rows_here = density.shape[1]
    grid_len = density.shape[2]
    outer_len = grid_len // RADIX
    local_cols = grid_len // wide_count
    tile_rows = rows_here // depth_count
    layer_field = density[0].reshape(rows_here, outer_len, RADIX)
    first_table = phase_table(outer_len, outer_len, outer_len, -1.0)
    partial_value = (
        product("rbc,ab->rac", layer_field, first_table[0]),
        product("rbc,ab->rac", layer_field, first_table[1]),
    )
    partial_value = times_table(partial_value, phase_table(outer_len, RADIX, grid_len, -1.0))
    partial_value = complex_product(
        "rab,bc->rac", partial_value, phase_table(RADIX, RADIX, RADIX, -1.0)
    )
    row_spectra = (
        partial_value[0].reshape(rows_here, wide_count, local_cols),
        partial_value[1].reshape(rows_here, wide_count, local_cols),
    )
    spectrum = column_forward(
        (
            lax.all_to_all(row_spectra[0], "wide", split_axis=1, concat_axis=0, tiled=True),
            lax.all_to_all(row_spectra[1], "wide", split_axis=1, concat_axis=0, tiled=True),
        )
    )
    position = lax.axis_index("wide") * local_cols + jnp.arange(local_cols, dtype=jnp.int32)
    index_x = position // RADIX + outer_len * (position % RADIX)
    index_y = (
        jnp.arange(outer_len, dtype=jnp.int32)[:, None]
        + outer_len * jnp.arange(RADIX, dtype=jnp.int32)[None, :]
    )
    full_x, odd_x = wavenumber(index_x, grid_len)
    full_y, odd_y = wavenumber(index_y, grid_len)
    full_x = full_x[None, None, :]
    odd_x = odd_x[None, None, :]
    full_y = full_y[:, :, None]
    odd_y = odd_y[:, :, None]
    squared = full_x * full_x + full_y * full_y
    magnitude = jnp.sqrt(squared)
    safe_square = jnp.where(squared > 0.0, squared, 1.0)
    safe_root = jnp.sqrt(safe_square)
    continuation = (
        2.0
        * math.pi
        / (grid_len * grid_len)
        * (1.0 - jnp.exp(-magnitude * layer_thick[0]))
        * jnp.exp(-magnitude * layer_top[0])
    )
    continued = (spectrum[0] * continuation, spectrum[1] * continuation)
    summed = lax.psum((continued[0], continued[1]), "depth")
    channels = channel_spectra(summed, full_x, full_y, odd_x, odd_y, safe_square, safe_root)
    partial_value = column_inverse_start(channels)
    row_share = outer_len // depth_count
    row_start = lax.axis_index("depth") * row_share
    back_table = phase_table(outer_len, outer_len, outer_len, 1.0)
    share_table = (
        lax.dynamic_slice_in_dim(back_table[0], row_start, row_share, 0),
        lax.dynamic_slice_in_dim(back_table[1], row_start, row_share, 0),
    )
    partial_value = complex_product("jbcd,ab->jacd", partial_value, share_table)
    row_blocks = (
        partial_value[0].reshape(3, wide_count, tile_rows, local_cols),
        partial_value[1].reshape(3, wide_count, tile_rows, local_cols),
    )
    row_fields = row_inverse(
        (
            lax.all_to_all(row_blocks[0], "wide", split_axis=1, concat_axis=3, tiled=True),
            lax.all_to_all(row_blocks[1], "wide", split_axis=1, concat_axis=3, tiled=True),
        )
    )
    gradient = ordered_channels(row_fields[0], row_fields[1]).reshape(6, tile_rows, grid_len)
    padded = padded_2(gradient, ((("depth", "wide"), 1),), 2)
    weight_table = weight_rows(QLEV)
    level_ids = jnp.arange(QLEV, dtype=jnp.int32)[None, :]
    frac_y = sample_frac[0, 0]
    frac_x = sample_frac[0, 1]
    weight_y = jnp.dot(
        (frac_y[:, None] == level_ids).astype(jnp.float32), weight_table, precision=HIGH
    )
    weight_x = jnp.dot(
        (frac_x[:, None] == level_ids).astype(jnp.float32), weight_table, precision=HIGH
    )
    base_y = jnp.where(frac_y < QLEV // 2, -1, 0).astype(jnp.int32)
    base_x = jnp.where(frac_x < QLEV // 2, -1, 0).astype(jnp.int32)
    tap_ids = jnp.arange(4, dtype=jnp.int32)[None, :]
    row_ids = (sample_row[0] + base_y + 1)[:, None] + tap_ids
    col_ids = ((sample_col[0] + base_x - 1)[:, None] + tap_ids) % grid_len
    neighbours = padded[:, row_ids[:, :, None], col_ids[:, None, :]]
    interpolated = jnp.einsum("csab,sa,sb->cs", neighbours, weight_y, weight_x, precision=HIGH)
    sample_count = sample_row.shape[1]
    capacity = max(2 * sample_count // wide_count, 2)
    slot_total = wide_count * capacity
    owner_ids = sample_owner[0, :, 0]
    owner_marks = (owner_ids[:, None] == jnp.arange(wide_count, dtype=jnp.int32)[None, :]).astype(
        jnp.int32
    )
    earlier = jnp.cumsum(owner_marks, axis=0) - owner_marks
    slot_ids = jnp.sum(earlier * owner_marks, axis=1)
    target = owner_ids * capacity + slot_ids
    placement = (target[:, None] == jnp.arange(slot_total, dtype=jnp.int32)[None, :]).astype(
        jnp.float32
    )
    outgoing = jnp.dot(interpolated, placement, precision=HIGH).reshape(6, wide_count, capacity)
    arrived = lax.all_to_all(outgoing, "wide", split_axis=1, concat_axis=1, tiled=True)
    return (gradient, arrived.reshape(6, 1, slot_total))


def solution(mesh):
    in_specs = (
        P("depth", "wide", None),
        P("depth"),
        P("depth"),
        P(("depth", "wide"), None),
        P(("depth", "wide"), None),
        P(("depth", "wide"), None, None),
        P(("depth", "wide"), None, None),
    )
    out_specs = (P(None, ("depth", "wide"), None), P(None, ("depth", "wide"), None))
    return jax.shard_map(
        per_device, mesh=mesh, in_specs=in_specs, out_specs=out_specs, check_vma=False
    )
```

profile of v0, /device:TPU:0, one launch (start us, length us, event | category | flops | bytes accessed | tf_op | source)
XLA Modules:
  0.0 1574.2 jit_solution(17820646528729374179)
XLA Ops:
  12.5 9.6 fusion.160
  22.1 13.1 subtract_bitcast_fusion.4
  35.2 14.0 fusion.44
  49.2 15.9 %fusion.71 = f32[512,32,128]{0,2,1:T(8,128)} fusion(f32[512,32,128]{0,2,1:T(8,128)} %fusion.44, f32[512,32,128]{2,1,0:T(8,128)S(1)} %get-tuple-element.26), kind=kOutput, calls=%fused_computation.98 | convolution fusion | flops 3223568384 | bytes 25165824 | tf_op jit(solution)/shard_map/rab,bc->rac/dot_general | solution.py:27
  65.1 9.6 copy.137
  79.8 18.6 %fusion.46 = f32[512,32,128]{0,2,1:T(8,128)S(1)} fusion(f32[512,32,128]{2,1,0:T(8,128)} %copy-done.5), kind=kOutput, calls=%fused_computation.69 | convolution fusion | flops 3221471232 | bytes 16777216 | tf_op jit(solution)/shard_map/rab,bc->rac/dot_general | solution.py:27
  98.5 21.9 %fusion.68 = f32[512,32,128]{0,2,1:T(8,128)} fusion(f32[512,32,128]{0,2,1:T(8,128)S(1)} %fusion.46, f32[512,32,128]{2,1,0:T(8,128)} %copy-done.2), kind=kOutput, calls=%fused_computation.97 | convolution fusion | flops 3223552000 | bytes 25165824 | tf_op jit(solution)/shard_map/rab,bc->rac/dot_general | solution.py:27
  120.3 9.1 copy.131
  129.4 44.9 %all-to-all-done.1 = f32[512,8,512]{2,0,1:T(8,128)} async-done(((f32[512,8,512]{2,0,1:T(8,128)}), f32[512,8,512]{2,0,1:T(8,128)}, u32[]{:S(2)}, u32[]{:S(2)}) %all-to-all-start.1) | async-done | bytes 8388640 | tf_op jit(solution)/shard_map/all_to_all | solution.py:172
  180.9 17.1 %fusion.36 = f32[32,128,512]{2,0,1:T(8,128)} fusion(f32[32,128,512]{2,1,0:T(8,128)} %bitcast.22), kind=kOutput, calls=%fused_computation.59 | convolution fusion | flops 805320704 | bytes 16777216 | tf_op jit(solution)/shard_map/bcd,ab->acd/dot_general | solution.py:27
  198.0 17.6 %fusion.38 = f32[32,128,512]{2,0,1:T(8,128)} fusion(f32[32,128,512]{2,1,0:T(8,128)} %bitcast.22), kind=kOutput, calls=%fused_computation.61 | convolution fusion | flops 805321728 | bytes 16777216 | tf_op jit(solution)/shard_map/bcd,ab->acd/dot_general | solution.py:27
  215.7 57.7 %all-to-all-done = f32[512,8,512]{2,0,1:T(8,128)} async-done(((f32[512,8,512]{2,0,1:T(8,128)}), f32[512,8,512]{2,0,1:T(8,128)}, u32[]{:S(2)}, u32[]{:S(2)}) %all-to-all-start) | async-done | bytes 8388640 | tf_op jit(solution)/shard_map/all_to_all | solution.py:171
  273.4 17.5 %fusion.42 = f32[32,128,512]{2,0,1:T(8,128)} fusion(f32[32,128,512]{2,1,0:T(8,128)} %bitcast.16), kind=kOutput, calls=%fused_computation.65 | convolution fusion | flops 805320704 | bytes 16777216 | tf_op jit(solution)/shard_map/bcd,ab->acd/dot_general | solution.py:27
  290.9 24.4 %multiply_subtract_fusion = (f32[32,128,512]{2,0,1:T(8,128)}, f32[32,128,512]{2,0,1:T(8,128)}) fusion(f32[32,128]{0,1:T(8,128)S(1)} %copy.142, f32[32,128]{0,1:T(8,128)S(1)} %copy.139, f32[32,128,512]{2,0,1:T(8,128)} %fusion.36, f32[32,128,512]{2,0,1:T(8,128)} %fusion.42, f32[32,128,512]{2,0,1:T(8,128)} %fusion.38, f32[32,128,512]{2,1,0:T(8,128)} %bitcast.16), kind=kOutput, calls=%fused_computation.48 | convolution fusion | flops 822098944 | bytes 50364416 | tf_op jit(solution)/shard_map/bcd,ab->acd/dot_general | solution.py:27
  315.3 18.1 %fusion.28 = f32[128,32,512]{2,0,1:T(8,128)S(1)} fusion(f32[32,128,512]{2,0,1:T(8,128)} %get-tuple-element.15), kind=kOutput, calls=%fused_computation.51 | convolution fusion | flops 3221454848 | bytes 16777216 | tf_op jit(solution)/shard_map/abd,bc->acd/dot_general | solution.py:27
  333.4 12.3 fusion.30
  345.8 18.2 %bitcast_multiply_fusion.5 = f32[32,128,512]{2,1,0:T(8,128)} fusion(f32[128,32,512]{2,0,1:T(8,128)S(1)} %fusion.30, f32[]{:T(128)} %bitcast.208, f32[]{:T(128)} %bitcast.210, f32[32,128]{1,0:T(8,128)S(1)} %get-tuple-element.40, f32[512]{0:T(512)S(1)} %fusion.224, f32[32,128,512]{2,0,1:T(8,128)S(1)} %bitcast.220), kind=kOutput, calls=%fused_computation.40 | convolution fusion | flops 3240329216 | bytes 25184264 | tf_op jit(solution)/shard_map/abd,bc->acd/dot_general | solution.py:27
  364.0 18.5 %bitcast_multiply_fusion.4 = f32[32,128,512]{2,1,0:T(8,128)} fusion(f32[128,32,512]{2,0,1:T(8,128)S(1)} %fusion.28, f32[]{:T(128)} %bitcast.209, f32[]{:T(128)} %bitcast.211, f32[32,128]{1,0:T(8,128)S(1)} %get-tuple-element.40, f32[512]{0:T(512)S(1)} %fusion.224, f32[32,128,512]{2,0,1:T(8,128)S(1)} %bitcast.220), kind=kOutput, calls=%fused_computation.39 | convolution fusion | flops 3240345600 | bytes 25184264 | tf_op jit(solution)/shard_map/abd,bc->acd/dot_general | solution.py:27
  382.8 563.3 %all-reduce.3.cloned.1.call-done = (f32[32,128,512]{2,1,0:T(8,128)}, f32[32,128,512]{2,1,0:T(8,128)}) async-done(((f32[32,128,512]{2,1,0:T(8,128)}, f32[32,128,512]{2,1,0:T(8,128)}), (f32[32,128,512]{2,1,0:T(8,128)}, f32[32,128,512]{2,1,0:T(8,128)})) %all-reduce.3.cloned.1.call-update) | async-done | bytes 16777232 | tf_op jit(solution)/shard_map/psum | solution.py:199
  946.1 21.0 %add_bitcast_fusion.1 = (f32[1,32,128,512]{3,2,1,0:T(8,128)}, f32[1,32,128,512]{3,2,1,0:T(8,128)S(1)}, f32[1,32,128,512]{3,2,1,0:T(8,128)}, f32[1,32,128,512]{3,...) fusion(f32[32,128,512]{2,1,0:T(8,128)} %get-tuple-element.10, ...), kind=kLoop, calls=%fused_computation.43 | loop fusion | flops 54525952 | bytes 67166208 | tf_op jit(solution)/shard_map/stack | solution.py:122
  967.1 34.1 %fusion.10 = f32[128,3,32,512]{3,0,2,1:T(8,128)} fusion(f32[1,32,128,512]{3,2,1,0:T(8,128)} %get-tuple-element.28, f32[1,32,128,512]{3,2,1,0:T(8,128)} %get-tuple-element.31, f32[1,32,128,512]{3,2,1,0:T(8,128)} %get-tuple-element.18), kind=kOutput, calls=%fused_computation.18 | convolution fusion | flops 9676488704 | bytes 50331648 | tf_op jit(solution)/shard_map/jabd,cb->jacd/dot_general | solution.py:27
  1001.2 29.1 %fusion.11 = f32[128,3,32,512]{3,0,2,1:T(8,128)} fusion(f32[1,32,128,512]{3,2,1,0:T(8,128)} %get-tuple-element.28, f32[1,32,128,512]{3,2,1,0:T(8,128)} %get-tuple-element.31, f32[1,32,128,512]{3,2,1,0:T(8,128)} %get-tuple-element.18), kind=kOutput, calls=%fused_computation.19 | convolution fusion | flops 9676488704 | bytes 50331648 | tf_op jit(solution)/shard_map/jabd,cb->jacd/dot_general | solution.py:27
  1030.4 28.4 %fusion.13 = f32[128,3,32,512]{3,0,2,1:T(8,128)} fusion(f32[1,32,128,512]{3,2,1,0:T(8,128)S(1)} %get-tuple-element.29, f32[1,32,128,512]{3,2,1,0:T(8,128)} %get-tuple-element.30, f32[1,32,128,512]{3,2,1,0:T(8,128)S(1)} %get-tuple-element.19), kind=kOutput, calls=%fused_computation.21 | convolution fusion | flops 9676488704 | bytes 50331648 | tf_op jit(solution)/shard_map/jabd,cb->jacd/dot_general | solution.py:27
  1058.8 60.9 %fusion = (f32[3,32,128,512]{3,2,1,0:T(8,128)}, f32[3,32,128,512]{3,2,1,0:T(8,128)}) fusion(f32[32,128]{1,0:T(8,128)S(1)} %fusion.189, f32[32,128]{1,0:T(8,128)S(1)} %get-tuple-element.43, f32[128,3,32,512]{3,0,2,1:T(8,128)} %fusion.10, f32[128,3,32,512]{3,0,2,1:T(8,128)} %fusion.13, f32[128,3,32,512]{3,0,2,1:T(8,128)} %fusion.11, ...), kind=kOutput, calls=%fused_computation.5 | convolution fusion | flops 9726820352 | bytes 151027712 | tf_op jit(solution)/shard_map/jabd,cb->jacd/dot_general | solution.py:27
  1119.6 34.6 %fusion.2 = f32[8,3,128,512]{3,0,2,1:T(8,128)} fusion(f32[3,32,128,512]{3,2,1,0:T(8,128)} %get-tuple-element.13, f32[32,32]{1,0:T(8,128)S(1)} %fusion.192, s32[]{:T(128)S(6)} %select_n.307), kind=kOutput, calls=%fused_computation.10 | convolution fusion | flops 603979776 | bytes 31461380 | tf_op jit(solution)/shard_map/jbcd,ab->jacd/dot_general | solution.py:27
  1154.2 26.1 %add_bitcast_fusion.4 = f32[3,8,128,512]{3,1,2,0:T(8,128)S(1)} fusion(f32[8,3,128,512]{3,0,2,1:T(8,128)} %fusion.2, f32[3,32,128,512]{3,2,1,0:T(8,128)S(1)} %copy-done, f32[32,32]{1,0:T(8,128)S(1)} %fusion.191, s32[]{:T(128)S(6)} %select_n.307), kind=kOutput, calls=%fused_computation.79 | convolution fusion | flops 605552640 | bytes 37752836 | tf_op jit(solution)/shard_map/jbcd,ab->jacd/dot_general | solution.py:27
  1180.4 6.3 copy.158
  1191.5 33.3 %fusion.4 = f32[8,3,128,512]{3,0,2,1:T(8,128)S(1)} fusion(f32[3,32,128,512]{3,2,1,0:T(8,128)} %get-tuple-element.13, f32[32,32]{1,0:T(8,128)S(1)} %fusion.191, s32[]{:T(128)S(6)} %select_n.307), kind=kOutput, calls=%fused_computation.12 | convolution fusion | flops 603979776 | bytes 31461380 | tf_op jit(solution)/shard_map/jbcd,ab->jacd/dot_general | solution.py:27
  1224.8 33.7 %subtract_bitcast_fusion.6 = f32[3,8,128,512]{3,1,2,0:T(8,128)S(1)} fusion(f32[8,3,128,512]{3,0,2,1:T(8,128)S(1)} %fusion.4, f32[3,32,128,512]{3,2,1,0:T(8,128)} %get-tuple-element.12, f32[32,32]{1,0:T(8,128)S(1)} %fusion.192, s32[]{:T(128)S(6)} %select_n.307), kind=kOutput, calls=%fused_computation.80 | convolution fusion | flops 605552640 | bytes 37752836 | tf_op jit(solution)/shard_map/jbcd,ab->jacd/dot_general | solution.py:27
  1275.2 9.1 copy.159
  1284.4 6.9 reshape.406
  1291.2 13.7 fusion.60
  1305.0 12.4 fusion.62
  1317.4 24.1 %all-to-all-done.2 = f32[3,8,128,512]{3,2,0,1:T(8,128)} async-done(((f32[3,8,128,512]{3,2,0,1:T(8,128)}), f32[3,8,128,512]{3,2,0,1:T(8,128)}, u32[]{:S(2)}, u32[]{:S(2)}) %all-to-all-start.2) | async-done | bytes 6291488 | tf_op jit(solution)/shard_map/all_to_all | solution.py:216
  1341.5 9.0 copy.154
  1350.5 6.9 reshape.405
  1357.4 13.9 fusion.66
  1371.3 15.5 multiply_subtract_fusion.1
  1386.8 9.3 fusion.52
  1396.1 9.7 fusion.54
  1405.8 13.0 subtract_bitcast_fusion.5
  1418.9 13.2 add_bitcast_fusion.3
  1432.0 7.2 reshape.407
  1445.1 7.7 copy.167
  1452.8 9.8 maximum_bitcast_fusion
  1472.2 6.5 pad_maximum_fusion.6
  1478.7 55.1 %gather_fusion = f32[4096,6]{0,1:T(8,128)S(1)} fusion(f32[6,132,4096]{2,0,1:T(8,128)} %pad_maximum_fusion.6, s32[4096]{0:T(1024)S(1)} %reshape.412), kind=kCustom, calls=%fused_computation | custom fusion | bytes 229376 | tf_op jit(solution)/shard_map/gather | solution.py:237
  1547.1 17.8 %copy.175 = f32[6,128,4096]{2,1,0:T(8,128)} copy(f32[6,128,4096]{2,0,1:T(8,128)} %copy-done.1) | data formatting | bytes 25165824
  (98 shorter events, 68.0 us)
Async XLA Ops:
  12.5 9.6 copy-start.6
  35.2 14.0 copy-start.5
  35.2 14.0 copy-start.2
  74.7 99.7 %all-to-all-start.1 = ((f32[512,8,512]{2,0,1:T(8,128)}), f32[512,8,512]{2,0,1:T(8,128)}, u32[]{:S(2)}, u32[]{:S(2)}) async-start(f32[512,8,512]{2,0,1:T(8,128)} %copy.137), calls=%async_computation.1 | async-start | bytes 16777216 | tf_op jit(solution)/shard_map/all_to_all | solution.py:172
  174.4 99.0 %all-to-all-start = ((f32[512,8,512]{2,0,1:T(8,128)}), f32[512,8,512]{2,0,1:T(8,128)}, u32[]{:S(2)}, u32[]{:S(2)}) async-start(f32[512,8,512]{2,0,1:T(8,128)} %copy.131), calls=%async_computation | async-start | bytes 16777216 | tf_op jit(solution)/shard_map/all_to_all | solution.py:171
  179.3 766.8 %all-reduce.3.cloned.1.call-start = ((), (), s32[]{:S(2)}) async-start(), calls=%async_computation.5 | async-start | bytes 33554432 | tf_op jit(solution)/shard_map/psum | solution.py:199
  315.3 18.1 %copy-start.7 = (f32[32,128,512]{2,0,1:T(8,128)S(1)}, f32[32,128,512]{2,0,1:T(8,128)}, u32[]{:S(2)}) copy-start(f32[32,128,512]{2,0,1:T(8,128)} %get-tuple-element.15) | copy-start | bytes 25165828
  315.3 30.5 %slice-start.2 = ((s8[8388608]{0:T(1024)(128)(4,1)}), s8[4194304]{0:T(1024)(128)(4,1)S(1)}, s32[]{:S(2)}) async-start(s8[8388608]{0:T(1024)(128)(4,1)} %bitcast.219), calls=%async_computation.8 | async-start | bytes 8388608
  333.4 12.4 slice-start.3
  967.1 63.2 %copy-start.3 = (f32[1,32,128,512]{3,2,1,0:T(8,128)}, f32[1,32,128,512]{3,2,1,0:T(8,128)S(1)}, u32[]{:S(2)}) copy-start(f32[1,32,128,512]{3,2,1,0:T(8,128)S(1)} %get-tuple-element.19) | copy-start | bytes 25165828
  967.1 63.2 %copy-start.4 = (f32[1,32,128,512]{3,2,1,0:T(8,128)}, f32[1,32,128,512]{3,2,1,0:T(8,128)S(1)}, u32[]{:S(2)}) copy-start(f32[1,32,128,512]{3,2,1,0:T(8,128)S(1)} %get-tuple-element.29) | copy-start | bytes 25165828
  1119.6 34.6 %copy-start = (f32[3,32,128,512]{3,2,1,0:T(8,128)S(1)}, f32[3,32,128,512]{3,2,1,0:T(8,128)}, u32[]{:S(2)}) copy-start(f32[3,32,128,512]{3,2,1,0:T(8,128)} %get-tuple-element.12) | copy-start | bytes 75497472
  1186.7 78.0 %all-to-all-start.3 = ((f32[3,8,128,512]{3,2,0,1:T(8,128)}), f32[3,8,128,512]{3,2,0,1:T(8,128)}, u32[]{:S(2)}, u32[]{:S(2)}) async-start(f32[3,8,128,512]{3,2,0,1:T(8,128)} %copy.158), calls=%async_computation.3 | async-start | bytes 12582912 | tf_op jit(solution)/shard_map/all_to_all | solution.py:217
  1264.7 5.1 copy-start.11
  1264.7 6.0 copy-start.12
  1264.7 6.0 copy-start.13
  1264.7 6.0 copy-start.14
  1264.8 76.7 %all-to-all-start.2 = ((f32[3,8,128,512]{3,2,0,1:T(8,128)}), f32[3,8,128,512]{3,2,0,1:T(8,128)}, u32[]{:S(2)}, u32[]{:S(2)}) async-start(f32[3,8,128,512]{3,2,0,1:T(8,128)} %copy.153), calls=%async_computation.2 | async-start | bytes 12582912 | tf_op jit(solution)/shard_map/all_to_all | solution.py:216
  1291.2 13.7 copy-start.8
  1357.4 13.9 copy-start.9
  1386.8 19.0 %slice-start = ((s8[6291456]{0:T(1024)(128)(4,1)}), s8[4194304]{0:T(1024)(128)(4,1)S(1)}, s32[]{:S(2)}) async-start(s8[6291456]{0:T(1024)(128)(4,1)} %bitcast.214), calls=%async_computation.6 | async-start | bytes 8388608
  1396.1 9.7 slice-start.1
  1439.2 5.8 copy-start.10
  1462.6 9.6 copy-start.1
  1462.7 9.5 collective-permute-start
  1462.8 9.5 collective-permute-start.1
  1543.5 21.4 %all-to-all-start.4 = ((f32[8,1,384]{2,1,0:T(1,128)}), f32[8,1,384]{2,1,0:T(1,128)S(1)}, u32[]{:S(2)}, u32[]{:S(2)}) async-start(f32[8,1,384]{2,1,0:T(1,128)} %reshape.439), calls=%async_computation.4 | async-start | bytes 24576 | tf_op jit(solution)/shard_map/all_to_all | solution.py:253
Sparse Core Ops, SparseCore 0:
  382.6 563.4 all-reduce.2
where the time goes:
time: 1580 us; the launch traced here: 1570 us
  waiting for transfers between devices  694 us (44%)
  matrix products  619 us (39%)
  local copies, waits for them, and re-layouts  172 us (11%)
  other arithmetic  44.5 us (3%)
  starting transfers between devices  29 us (2%)
  between operations  16.3 us (1%)
    dot_general x30, matrix products, product(): return jnp.einsum(formula, operand_a, operand_b, precision=HIGH)  618 us
    psum x1, waiting for transfers between devices, per_device(): summed = lax.psum((continued[0], continued[1]), 'depth')  563 us
    gather x2, local copies, waits for them, and re-layouts, per_device(): neighbours = padded[:, row_ids[:, :, None], col_ids[:, None, :]]  59.2 us
    all_to_all x1, waiting for transfers between devices, per_device(): lax.all_to_all(row_spectra[0], 'wide', split_axis=1, concat_axis=0, tiled...  57.7 us
    all_to_all x1, waiting for transfers between devices, per_device(): lax.all_to_all(row_spectra[1], 'wide', split_axis=1, concat_axis=0, tiled...  44.9 us
  transfers between devices with their start and end apart: 8, of which 5 were waited for; matrix products, arithmetic and copies ran while one was open for 14% of the time, Pallas kernels for 0%

commit v1 on v0

--- a/solution.py
+++ b/solution.py
@@ -168,7 +168,15 @@
     )
     spectrum = column_forward(
         (
-            lax.all_to_all(row_spectra[0], "wide", split_axis=1, concat_axis=0, tiled=True),
+            jnp.concatenate(
+                lax.all_to_all(
+                    jnp.stack(jnp.split(row_spectra[0], lax.axis_size("wide"), axis=1)),
+                    "wide",
+                    0,
+                    0,
+                ),
+                axis=0,
+            ),
             lax.all_to_all(row_spectra[1], "wide", split_axis=1, concat_axis=0, tiled=True),
         )
     )

time: 1580 us -> 1590 us (level)
  local copies, waits for them, and re-layouts: 172 us -> 196 us
  waiting for transfers between devices: 694 us -> 673 us
    unnamed x43 -> x66, local copies, waits for them, and re-layouts: 26.3 us -> 55.5 us
    all_to_all x1, waiting for transfers between devices: 44.9 us -> 24.1 us  [per_device(): lax.all_to_all(row_spectra[1], 'wide', split_axis=1, concat_axis=0, tiled...]
  transfers between devices with their start and end apart: 8 -> 8, of which waited for: 5 -> 5; matrix products, arithmetic and copies ran while one was open for 14% -> 16% of each run, Pallas kernels for 0% -> 0%
where the time goes in v1:
time: 1590 us; the launch traced here: 1580 us
  waiting for transfers between devices  673 us (42%)
  matrix products  616 us (39%)
  local copies, waits for them, and re-layouts  196 us (12%)
  other arithmetic  44.5 us (3%)
  starting transfers between devices  29.2 us (2%)
  between operations  16.3 us (1%)
    dot_general x30, matrix products, product(): return jnp.einsum(formula, operand_a, operand_b, precision=HIGH)  615 us
    psum x1, waiting for transfers between devices, per_device(): summed = lax.psum((continued[0], continued[1]), 'depth')  563 us
    gather x2, local copies, waits for them, and re-layouts, per_device(): neighbours = padded[:, row_ids[:, :, None], col_ids[:, None, :]]  59.8 us
    all_to_all x1, waiting for transfers between devices, per_device(): lax.all_to_all(jnp.stack(jnp.split(row_spectra[0], lax.axis_size('wide'),...  57.7 us
    unnamed x66, local copies, waits for them, and re-layouts  55.5 us
  transfers between devices with their start and end apart: 8, of which 5 were waited for; matrix products, arithmetic and copies ran while one was open for 16% of the time, Pallas kernels for 0%

profile of v1, /device:TPU:0, one launch (start us, length us, event | category | flops | bytes accessed | tf_op | source)
XLA Modules:
  0.0 1575.2 jit_solution(10975354988440490705)
XLA Ops:
  12.5 9.6 fusion.160
  22.1 13.1 subtract_bitcast_fusion.4
  35.2 14.0 fusion.44
  49.1 15.9 %fusion.71 = f32[512,32,128]{0,2,1:T(8,128)} fusion(f32[512,32,128]{0,2,1:T(8,128)} %fusion.44, f32[512,32,128]{2,1,0:T(8,128)S(1)} %get-tuple-element.26), kind=kOutput, calls=%fused_computation.98 | convolution fusion | flops 3223568384 | bytes 25165824 | tf_op jit(solution)/shard_map/rab,bc->rac/dot_general | solution.py:27
  65.1 9.5 copy.158
  79.8 18.5 %fusion.46 = f32[512,32,128]{0,2,1:T(8,128)S(1)} fusion(f32[512,32,128]{2,1,0:T(8,128)} %copy-done.5), kind=kOutput, calls=%fused_computation.69 | convolution fusion | flops 3221471232 | bytes 16777216 | tf_op jit(solution)/shard_map/rab,bc->rac/dot_general | solution.py:27
  98.3 19.2 %fusion.68 = f32[512,32,128]{0,2,1:T(8,128)S(1)} fusion(f32[512,32,128]{0,2,1:T(8,128)S(1)} %fusion.46, f32[512,32,128]{2,1,0:T(8,128)} %copy-done.2), kind=kOutput, calls=%fused_computation.97 | convolution fusion | flops 3223552000 | bytes 25165824 | tf_op jit(solution)/shard_map/rab,bc->rac/dot_general | solution.py:27
  150.4 24.1 %all-to-all-done.1 = f32[512,8,512]{2,0,1:T(8,128)} async-done(((f32[512,8,512]{2,0,1:T(8,128)}), f32[512,8,512]{2,0,1:T(8,128)}, u32[]{:S(2)}, u32[]{:S(2)}) %all-to-all-start.1) | async-done | bytes 8388640 | tf_op jit(solution)/shard_map/all_to_all | solution.py:180
  181.2 17.1 %fusion.36 = f32[32,128,512]{2,0,1:T(8,128)} fusion(f32[32,128,512]{2,1,0:T(8,128)} %bitcast.28), kind=kOutput, calls=%fused_computation.59 | convolution fusion | flops 805320704 | bytes 16777216 | tf_op jit(solution)/shard_map/bcd,ab->acd/dot_general | solution.py:27
  198.4 17.6 %fusion.38 = f32[32,128,512]{2,0,1:T(8,128)} fusion(f32[32,128,512]{2,1,0:T(8,128)} %bitcast.28), kind=kOutput, calls=%fused_computation.61 | convolution fusion | flops 805321728 | bytes 16777216 | tf_op jit(solution)/shard_map/bcd,ab->acd/dot_general | solution.py:27
  216.0 57.7 %all-to-all-done = f32[8,512,1,512]{3,1,2,0:T(8,128)} async-done(((f32[8,512,1,512]{3,1,2,0:T(8,128)}), f32[8,512,1,512]{3,1,2,0:T(8,128)}, u32[]{:S(2)}, u32[]{:S(2)}) %all-to-all-start) | async-done | bytes 8388640 | tf_op jit(solution)/shard_map/all_to_all | solution.py:172
  273.7 17.7 %fusion.42 = f32[32,128,512]{2,0,1:T(8,128)} fusion(f32[32,128,512]{2,1,0:T(8,128)} %bitcast.22), kind=kOutput, calls=%fused_computation.65 | convolution fusion | flops 805320704 | bytes 16777216 | tf_op jit(solution)/shard_map/bcd,ab->acd/dot_general | solution.py:27
  291.4 24.4 %multiply_subtract_fusion = (f32[32,128,512]{2,0,1:T(8,128)}, f32[32,128,512]{2,0,1:T(8,128)}) fusion(f32[32,128]{0,1:T(8,128)S(1)} %copy.163, f32[32,128]{0,1:T(8,128)S(1)} %copy.160, f32[32,128,512]{2,0,1:T(8,128)} %fusion.36, f32[32,128,512]{2,0,1:T(8,128)} %fusion.42, f32[32,128,512]{2,0,1:T(8,128)} %fusion.38, f32[32,128,512]{2,1,0:T(8,128)} %bitcast.22), kind=kOutput, calls=%fused_computation.48 | convolution fusion | flops 822098944 | bytes 50364416 | tf_op jit(solution)/shard_map/bcd,ab->acd/dot_general | solution.py:27
  315.8 18.1 %fusion.28 = f32[128,32,512]{2,0,1:T(8,128)S(1)} fusion(f32[32,128,512]{2,0,1:T(8,128)} %get-tuple-element.15), kind=kOutput, calls=%fused_computation.51 | convolution fusion | flops 3221454848 | bytes 16777216 | tf_op jit(solution)/shard_map/abd,bc->acd/dot_general | solution.py:27
  333.9 12.3 fusion.30
  346.3 18.2 %bitcast_multiply_fusion.5 = f32[32,128,512]{2,1,0:T(8,128)} fusion(f32[128,32,512]{2,0,1:T(8,128)S(1)} %fusion.30, f32[]{:T(128)} %bitcast.220, f32[]{:T(128)} %bitcast.222, f32[32,128]{1,0:T(8,128)S(1)} %get-tuple-element.48, f32[512]{0:T(512)S(1)} %fusion.224, f32[32,128,512]{2,0,1:T(8,128)S(1)} %bitcast.232), kind=kOutput, calls=%fused_computation.40 | convolution fusion | flops 3240329216 | bytes 25184264 | tf_op jit(solution)/shard_map/abd,bc->acd/dot_general | solution.py:27
  364.5 18.5 %bitcast_multiply_fusion.4 = f32[32,128,512]{2,1,0:T(8,128)} fusion(f32[128,32,512]{2,0,1:T(8,128)S(1)} %fusion.28, f32[]{:T(128)} %bitcast.221, f32[]{:T(128)} %bitcast.223, f32[32,128]{1,0:T(8,128)S(1)} %get-tuple-element.48, f32[512]{0:T(512)S(1)} %fusion.224, f32[32,128,512]{2,0,1:T(8,128)S(1)} %bitcast.232), kind=kOutput, calls=%fused_computation.39 | convolution fusion | flops 3240345600 | bytes 25184264 | tf_op jit(solution)/shard_map/abd,bc->acd/dot_general | solution.py:27
  383.3 563.2 %all-reduce.3.cloned.1.call-done = (f32[32,128,512]{2,1,0:T(8,128)}, f32[32,128,512]{2,1,0:T(8,128)}) async-done(((f32[32,128,512]{2,1,0:T(8,128)}, f32[32,128,512]{2,1,0:T(8,128)}), (f32[32,128,512]{2,1,0:T(8,128)}, f32[32,128,512]{2,1,0:T(8,128)})) %all-reduce.3.cloned.1.call-update) | async-done | bytes 16777232 | tf_op jit(solution)/shard_map/psum | solution.py:207
  946.5 21.0 %add_bitcast_fusion.1 = (f32[1,32,128,512]{3,2,1,0:T(8,128)}, f32[1,32,128,512]{3,2,1,0:T(8,128)S(1)}, f32[1,32,128,512]{3,2,1,0:T(8,128)}, f32[1,32,128,512]{3,...) fusion(f32[32,128,512]{2,1,0:T(8,128)} %get-tuple-element.10, ...), kind=kLoop, calls=%fused_computation.43 | loop fusion | flops 54525952 | bytes 67166208 | tf_op jit(solution)/shard_map/stack | solution.py:122
  967.5 34.1 %fusion.10 = f32[128,3,32,512]{3,0,2,1:T(8,128)} fusion(f32[1,32,128,512]{3,2,1,0:T(8,128)} %get-tuple-element.28, f32[1,32,128,512]{3,2,1,0:T(8,128)} %get-tuple-element.31, f32[1,32,128,512]{3,2,1,0:T(8,128)} %get-tuple-element.18), kind=kOutput, calls=%fused_computation.18 | convolution fusion | flops 9676488704 | bytes 50331648 | tf_op jit(solution)/shard_map/jabd,cb->jacd/dot_general | solution.py:27
  1001.6 29.1 %fusion.11 = f32[128,3,32,512]{3,0,2,1:T(8,128)} fusion(f32[1,32,128,512]{3,2,1,0:T(8,128)} %get-tuple-element.28, f32[1,32,128,512]{3,2,1,0:T(8,128)} %get-tuple-element.31, f32[1,32,128,512]{3,2,1,0:T(8,128)} %get-tuple-element.18), kind=kOutput, calls=%fused_computation.19 | convolution fusion | flops 9676488704 | bytes 50331648 | tf_op jit(solution)/shard_map/jabd,cb->jacd/dot_general | solution.py:27
  1030.8 28.4 %fusion.13 = f32[128,3,32,512]{3,0,2,1:T(8,128)} fusion(f32[1,32,128,512]{3,2,1,0:T(8,128)S(1)} %get-tuple-element.29, f32[1,32,128,512]{3,2,1,0:T(8,128)} %get-tuple-element.30, f32[1,32,128,512]{3,2,1,0:T(8,128)S(1)} %get-tuple-element.19), kind=kOutput, calls=%fused_computation.21 | convolution fusion | flops 9676488704 | bytes 50331648 | tf_op jit(solution)/shard_map/jabd,cb->jacd/dot_general | solution.py:27
  1059.2 60.9 %fusion = (f32[3,32,128,512]{3,2,1,0:T(8,128)}, f32[3,32,128,512]{3,2,1,0:T(8,128)}) fusion(f32[32,128]{1,0:T(8,128)S(1)} %fusion.189, f32[32,128]{1,0:T(8,128)S(1)} %get-tuple-element.51, f32[128,3,32,512]{3,0,2,1:T(8,128)} %fusion.10, f32[128,3,32,512]{3,0,2,1:T(8,128)} %fusion.13, f32[128,3,32,512]{3,0,2,1:T(8,128)} %fusion.11, ...), kind=kOutput, calls=%fused_computation.5 | convolution fusion | flops 9726820352 | bytes 151027712 | tf_op jit(solution)/shard_map/jabd,cb->jacd/dot_general | solution.py:27
  1120.1 34.6 %fusion.2 = f32[8,3,128,512]{3,0,2,1:T(8,128)} fusion(f32[3,32,128,512]{3,2,1,0:T(8,128)} %get-tuple-element.13, f32[32,32]{1,0:T(8,128)S(1)} %fusion.192, s32[]{:T(128)S(6)} %select_n.307), kind=kOutput, calls=%fused_computation.10 | convolution fusion | flops 603979776 | bytes 31461380 | tf_op jit(solution)/shard_map/jbcd,ab->jacd/dot_general | solution.py:27
  1154.7 26.1 %add_bitcast_fusion.4 = f32[3,8,128,512]{3,1,2,0:T(8,128)S(1)} fusion(f32[8,3,128,512]{3,0,2,1:T(8,128)} %fusion.2, f32[3,32,128,512]{3,2,1,0:T(8,128)S(1)} %copy-done, f32[32,32]{1,0:T(8,128)S(1)} %fusion.191, s32[]{:T(128)S(6)} %select_n.307), kind=kOutput, calls=%fused_computation.79 | convolution fusion | flops 605552640 | bytes 37752836 | tf_op jit(solution)/shard_map/jbcd,ab->jacd/dot_general | solution.py:27
  1180.8 6.3 copy.179
  1191.9 33.3 %fusion.4 = f32[8,3,128,512]{3,0,2,1:T(8,128)S(1)} fusion(f32[3,32,128,512]{3,2,1,0:T(8,128)} %get-tuple-element.13, f32[32,32]{1,0:T(8,128)S(1)} %fusion.191, s32[]{:T(128)S(6)} %select_n.307), kind=kOutput, calls=%fused_computation.12 | convolution fusion | flops 603979776 | bytes 31461380 | tf_op jit(solution)/shard_map/jbcd,ab->jacd/dot_general | solution.py:27
  1225.2 33.7 %subtract_bitcast_fusion.6 = f32[3,8,128,512]{3,1,2,0:T(8,128)S(1)} fusion(f32[8,3,128,512]{3,0,2,1:T(8,128)S(1)} %fusion.4, f32[3,32,128,512]{3,2,1,0:T(8,128)} %get-tuple-element.12, f32[32,32]{1,0:T(8,128)S(1)} %fusion.192, s32[]{:T(128)S(6)} %select_n.307), kind=kOutput, calls=%fused_computation.80 | convolution fusion | flops 605552640 | bytes 37752836 | tf_op jit(solution)/shard_map/jbcd,ab->jacd/dot_general | solution.py:27
  1258.9 6.2 copy.174
  1275.7 9.1 copy.180
  1284.8 6.9 reshape.401
  1291.7 13.7 fusion.60
  1305.4 12.4 fusion.62
  1317.8 24.1 %all-to-all-done.2 = f32[3,8,128,512]{3,2,0,1:T(8,128)} async-done(((f32[3,8,128,512]{3,2,0,1:T(8,128)}), f32[3,8,128,512]{3,2,0,1:T(8,128)}, u32[]{:S(2)}, u32[]{:S(2)}) %all-to-all-start.2) | async-done | bytes 6291488 | tf_op jit(solution)/shard_map/all_to_all | solution.py:224
  1341.9 9.0 copy.175
  1350.9 6.9 reshape.400
  1357.8 13.9 fusion.66
  1371.7 15.5 multiply_subtract_fusion.1
  1387.3 9.3 fusion.52
  1396.6 9.7 fusion.54
  1406.3 13.0 subtract_bitcast_fusion.5
  1419.3 13.2 add_bitcast_fusion.3
  1432.5 7.2 reshape.402
  1445.5 7.7 copy.188
  1453.2 9.8 maximum_bitcast_fusion
  1472.7 6.5 pad_maximum_fusion.6
  1479.2 55.7 %gather_fusion = f32[4096,6]{0,1:T(8,128)S(1)} fusion(f32[6,132,4096]{2,0,1:T(8,128)} %pad_maximum_fusion.6, s32[4096]{0:T(1024)S(1)} %reshape.407), kind=kCustom, calls=%fused_computation | custom fusion | bytes 229376 | tf_op jit(solution)/shard_map/gather | solution.py:245
  1548.1 17.8 %copy.196 = f32[6,128,4096]{2,1,0:T(8,128)} copy(f32[6,128,4096]{2,0,1:T(8,128)} %copy-done.1) | data formatting | bytes 25165824
  (122 shorter events, 94.8 us)
Async XLA Ops:
  12.5 9.6 copy-start.6
  35.1 14.0 copy-start.5
  35.2 14.0 copy-start.2
  74.6 99.8 %all-to-all-start.1 = ((f32[512,8,512]{2,0,1:T(8,128)}), f32[512,8,512]{2,0,1:T(8,128)}, u32[]{:S(2)}, u32[]{:S(2)}) async-start(f32[512,8,512]{2,0,1:T(8,128)} %copy.158), calls=%async_computation.1 | async-start | bytes 16777216 | tf_op jit(solution)/shard_map/all_to_all | solution.py:180
  134.2 14.0 copy-start.12
  135.5 13.8 copy-start.11
  136.8 9.3 copy-start.14
  136.8 10.4 copy-start.13
  174.4 99.3 %all-to-all-start = ((f32[8,512,1,512]{3,1,2,0:T(8,128)}), f32[8,512,1,512]{3,1,2,0:T(8,128)}, u32[]{:S(2)}, u32[]{:S(2)}) async-start(f32[8,512,1,512]{3,1,2,0:T(8,128)} %bitcast_dynamic-update-slice_fusion), calls=%async_computation | async-start | bytes 16777216 | tf_op jit(solution)/shard_map/all_to_all | solution.py:172
  179.6 766.8 %all-reduce.3.cloned.1.call-start = ((), (), s32[]{:S(2)}) async-start(), calls=%async_computation.5 | async-start | bytes 33554432 | tf_op jit(solution)/shard_map/psum | solution.py:207
  315.8 18.1 %copy-start.7 = (f32[32,128,512]{2,0,1:T(8,128)S(1)}, f32[32,128,512]{2,0,1:T(8,128)}, u32[]{:S(2)}) copy-start(f32[32,128,512]{2,0,1:T(8,128)} %get-tuple-element.15) | copy-start | bytes 25165828
  315.8 30.5 %slice-start.2 = ((s8[8388608]{0:T(1024)(128)(4,1)}), s8[4194304]{0:T(1024)(128)(4,1)S(1)}, s32[]{:S(2)}) async-start(s8[8388608]{0:T(1024)(128)(4,1)} %bitcast.231), calls=%async_computation.8 | async-start | bytes 8388608
  333.9 12.4 slice-start.3
  967.5 63.3 %copy-start.3 = (f32[1,32,128,512]{3,2,1,0:T(8,128)}, f32[1,32,128,512]{3,2,1,0:T(8,128)S(1)}, u32[]{:S(2)}) copy-start(f32[1,32,128,512]{3,2,1,0:T(8,128)S(1)} %get-tuple-element.19) | copy-start | bytes 25165828
  967.5 63.3 %copy-start.4 = (f32[1,32,128,512]{3,2,1,0:T(8,128)}, f32[1,32,128,512]{3,2,1,0:T(8,128)S(1)}, u32[]{:S(2)}) copy-start(f32[1,32,128,512]{3,2,1,0:T(8,128)S(1)} %get-tuple-element.29) | copy-start | bytes 25165828
  1120.1 34.6 %copy-start = (f32[3,32,128,512]{3,2,1,0:T(8,128)S(1)}, f32[3,32,128,512]{3,2,1,0:T(8,128)}, u32[]{:S(2)}) copy-start(f32[3,32,128,512]{3,2,1,0:T(8,128)} %get-tuple-element.12) | copy-start | bytes 75497472
  1187.2 78.0 %all-to-all-start.3 = ((f32[3,8,128,512]{3,2,0,1:T(8,128)}), f32[3,8,128,512]{3,2,0,1:T(8,128)}, u32[]{:S(2)}, u32[]{:S(2)}) async-start(f32[3,8,128,512]{3,2,0,1:T(8,128)} %copy.179), calls=%async_computation.3 | async-start | bytes 12582912 | tf_op jit(solution)/shard_map/all_to_all | solution.py:225
  1265.2 5.1 copy-start.15
  1265.2 6.0 copy-start.16
  1265.2 6.0 copy-start.17
  1265.2 6.0 copy-start.18
  1265.2 76.7 %all-to-all-start.2 = ((f32[3,8,128,512]{3,2,0,1:T(8,128)}), f32[3,8,128,512]{3,2,0,1:T(8,128)}, u32[]{:S(2)}, u32[]{:S(2)}) async-start(f32[3,8,128,512]{3,2,0,1:T(8,128)} %copy.174), calls=%async_computation.2 | async-start | bytes 12582912 | tf_op jit(solution)/shard_map/all_to_all | solution.py:224
  1291.7 13.7 copy-start.8
  1357.8 13.9 copy-start.9
  1387.3 19.0 %slice-start = ((s8[6291456]{0:T(1024)(128)(4,1)}), s8[4194304]{0:T(1024)(128)(4,1)S(1)}, s32[]{:S(2)}) async-start(s8[6291456]{0:T(1024)(128)(4,1)} %bitcast.226), calls=%async_computation.6 | async-start | bytes 8388608
  1396.6 9.7 slice-start.1
  1439.7 5.8 copy-start.10
  1463.1 9.6 copy-start.1
  1463.1 9.5 collective-permute-start
  1463.2 9.5 collective-permute-start.1
  1544.5 21.4 %all-to-all-start.4 = ((f32[8,1,384]{2,1,0:T(1,128)}), f32[8,1,384]{2,1,0:T(1,128)S(1)}, u32[]{:S(2)}, u32[]{:S(2)}) async-start(f32[8,1,384]{2,1,0:T(1,128)} %reshape.434), calls=%async_computation.4 | async-start | bytes 24576 | tf_op jit(solution)/shard_map/all_to_all | solution.py:261
Sparse Core Ops, SparseCore 0:
  383.1 563.3 all-reduce.2
